TPU v7x, 32 devices: a whole 2x2x4 slice. The times are simulated.
32 devices in a mesh: ctx: 8 (over y, x, core), tp: 4 (over z).
Axes of the slice: x: 2, y: 2, z: 4, core: 2. Of those that a mesh axis runs over, the one named last changes fastest.
Arguments:
- query_mr: bfloat16 [2048, 8192], P('ctx', 'tp'), may hold values from -6 to 6
- key_mr: bfloat16 [2048, 8192], P('ctx', 'tp'), may hold values from -6 to 6
- value_mr: bfloat16 [2048, 8192], P('ctx', 'tp'), may hold values from -6 to 6
- query_li: bfloat16 [2048, 8192], P('ctx', 'tp'), may hold values from -6 to 6
- key_li: bfloat16 [2048, 8192], P('ctx', 'tp'), may hold values from -6 to 6
- cotangent: bfloat16 [2048, 8192], P('ctx', 'tp'), may hold values from -6 to 6
- mr_taps: float32 [128, 8192], P(None, 'tp'), may hold values from -0.5 to 0.5
- decay_rates: float32 [8], replicated, may hold values from 4.8828126e-05 to 0.03
- residues: float32 [8, 8192], P(None, 'tp'), may hold values from -2 to 2
Outputs:
- grad_query_mr: bfloat16 [2048, 8192], P('ctx', 'tp')
- grad_key_mr: bfloat16 [2048, 8192], P('ctx', 'tp')
- grad_value_mr: bfloat16 [2048, 8192], P('ctx', 'tp')
- grad_query_li: bfloat16 [2048, 8192], P('ctx', 'tp')
- grad_key_li: bfloat16 [2048, 8192], P('ctx', 'tp')
- grad_taps: float32 [128, 8192], P(None, 'tp')
- grad_residues: float32 [8, 8192], P(None, 'tp')
All inputs are finite; a program needn't handle non-finite values.
Results may differ from a plain program's by a relative error of at most 0.001.
Values may be sent and summed in bfloat16 or wider, within the bound.
A program may use at most 128 MiB of HBM per device.

v0:
```python
import math
import jax
import jax.numpy as jnp
from jax import lax
from jax.sharding import PartitionSpec as P

BLOCK = 128
highest = lax.Precision.HIGHEST


def from_behind(value, axis, by):
    size = lax.axis_size(axis)
    pairs = [(i, i + by) for i in range(size) if 0 <= i + by < size]
    return lax.ppermute(value, axis, pairs)


def depthwise(signal, kernel):
    channels = signal.shape[1]
    output = lax.conv_general_dilated(
        signal[None],
        kernel[:, None, :],
        (1,),
        "VALID",
        dimension_numbers=("NWC", "WIO", "NWC"),
        feature_group_count=channels,
        precision=highest,
    )
    return output[0]


def linked(earlier, later):
    return (earlier[0] * later[1] + later[0], earlier[1] * later[1])


def modal_terms(inputs, cotangents, decay_rates, residues, block_len):
    length, channels = inputs.shape
    blocks = length // block_len
    in_blocks = inputs.reshape(blocks, block_len, channels)
    co_blocks = cotangents.reshape(blocks, block_len, channels)
    places = jnp.arange(block_len, dtype=jnp.float32)
    offsets = places[:, None] - places[None, :]
    modes = decay_rates.shape[0]

    def one_mode(mode, state):
        conv_sum, back_sum, residue_grad, end_rows, start_rows = state
        decay_rate = decay_rates[mode]
        residue_row = lax.dynamic_index_in_dim(residues, mode, 0, keepdims=False)
        mode_scale = jnp.sqrt(-jnp.expm1(-2.0 * decay_rate))
        toeplitz = jnp.where(
            offsets >= 0.0, mode_scale * jnp.exp(-decay_rate * jnp.maximum(offsets, 0.0)), 0.0
        )
        block_pows = jnp.full((blocks, 1), jnp.exp(-decay_rate * block_len), jnp.float32)
        forward = jnp.einsum("tj,bjc->btc", toeplitz, in_blocks, precision=highest)
        backward = jnp.einsum("jt,bjc->btc", toeplitz, co_blocks, precision=highest)
        forward_incl = lax.associative_scan(linked, (forward[:, -1], block_pows))[0]
        backward_incl = lax.associative_scan(linked, (backward[:, 0], block_pows), reverse=True)[0]
        zero_row = jnp.zeros((1, channels), jnp.float32)
        forward_in = jnp.concatenate([zero_row, forward_incl[:-1]], 0)
        backward_in = jnp.concatenate([backward_incl[1:], zero_row], 0)
        lead_pows = jnp.exp(-decay_rate * (places + 1.0))
        tail_pows = jnp.exp(-decay_rate * (block_len - places))
        states = (forward + lead_pows[None, :, None] * forward_in[:, None, :]).reshape(
            length, channels
        )
        reverse_states = (backward + tail_pows[None, :, None] * backward_in[:, None, :]).reshape(
            length, channels
        )
        conv_sum = conv_sum + residue_row[None, :] * states
        back_sum = back_sum + residue_row[None, :] * reverse_states
        residue_grad = lax.dynamic_update_index_in_dim(
            residue_grad, jnp.sum(inputs * reverse_states, 0), mode, 0
        )
        end_rows = lax.dynamic_update_index_in_dim(end_rows, states[length - 1], mode, 0)
        start_rows = lax.dynamic_update_index_in_dim(start_rows, reverse_states[0], mode, 0)
        return (conv_sum, back_sum, residue_grad, end_rows, start_rows)

    zero_field = jnp.zeros((length, channels), jnp.float32)
    zero_modes = jnp.zeros((modes, channels), jnp.float32)
    return lax.fori_loop(
        0, modes, one_mode, (zero_field, zero_field, zero_modes, zero_modes, zero_modes)
    )


def per_device(
    query_mr, key_mr, value_mr, query_li, key_li, cotangent, mr_taps, decay_rates, residues
):
    length, channels = query_mr.shape
    taps_len = mr_taps.shape[0]
    rim_rows = taps_len - 1
    devices_ctx = lax.axis_size("ctx")
    seq_len = length * devices_ctx
    prior_key, prior_value = from_behind(
        (key_mr[length - rim_rows :], value_mr[length - rim_rows :]), "ctx", 1
    )
    key_first = key_mr.astype(jnp.float32)
    value_first = value_mr.astype(jnp.float32)
    query_first = query_mr.astype(jnp.float32)
    mixed_in = jnp.concatenate([prior_key, key_mr], 0).astype(jnp.float32) * jnp.concatenate(
        [prior_value, value_mr], 0
    ).astype(jnp.float32)
    mr_conv = depthwise(mixed_in, mr_taps[::-1])
    mr_out = query_first * mr_conv
    key_second = key_li.astype(jnp.float32)
    cotan = cotangent.astype(jnp.float32)
    li_input = key_second * mr_out
    li_cotan = cotan * query_li.astype(jnp.float32)
    regrouped = lax.all_to_all(
        jnp.stack([li_input, li_cotan]), "ctx", split_axis=2, concat_axis=1, tiled=True
    )
    piece_cols = channels // devices_ctx
    local_residues = lax.dynamic_slice_in_dim(
        residues, lax.axis_index("ctx") * piece_cols, piece_cols, 1
    )
    conv_seq, back_seq, residue_piece, unused_ends, unused_starts = modal_terms(
        regrouped[0], regrouped[1], decay_rates, local_residues, BLOCK
    )
    returned = lax.all_to_all(
        jnp.stack([conv_seq, back_seq]), "ctx", split_axis=1, concat_axis=2, tiled=True
    )
    li_conv = returned[0]
    li_back = returned[1]
    residue_sum = lax.all_gather(residue_piece, "ctx", axis=1, tiled=True)
    grad_query_li = (cotan * li_conv).astype(jnp.bfloat16)
    grad_key_li = (mr_out * li_back).astype(jnp.bfloat16)
    mr_grad = cotan + key_second * li_back
    grad_query_mr = (mr_grad * mr_conv).astype(jnp.bfloat16)
    mr_cotan = mr_grad * query_first
    next_rows = from_behind(mr_cotan[:rim_rows], "ctx", -1)
    mixed_grad = depthwise(jnp.concatenate([mr_cotan, next_rows], 0), mr_taps)
    grad_key_mr = (mixed_grad * value_first).astype(jnp.bfloat16)
    grad_value_mr = (mixed_grad * key_first).astype(jnp.bfloat16)
    tap_part = depthwise(mixed_in, mr_cotan)[::-1]
    tap_sum = lax.psum(tap_part, "ctx")
    factor = 1.0 / math.sqrt(seq_len)
    return (
        grad_query_mr,
        grad_key_mr,
        grad_value_mr,
        grad_query_li,
        grad_key_li,
        tap_sum * factor,
        residue_sum * factor,
    )


def solution(mesh):
    placed = (
        P("ctx", "tp"),
        P("ctx", "tp"),
        P("ctx", "tp"),
        P("ctx", "tp"),
        P("ctx", "tp"),
        P("ctx", "tp"),
        P(None, "tp"),
        P(),
        P(None, "tp"),
    )
    return jax.shard_map(
        per_device,
        mesh=mesh,
        in_specs=placed,
        out_specs=(
            P("ctx", "tp"),
            P("ctx", "tp"),
            P("ctx", "tp"),
            P("ctx", "tp"),
            P("ctx", "tp"),
            P(None, "tp"),
            P(None, "tp"),
        ),
        check_vma=False,
    )
```

profile of v0, /device:TPU:0, one launch (start us, length us, event | category | flops | bytes accessed | tf_op | source)
XLA Modules:
  0.0 570.9 jit_solution(17721856543120809470)
XLA Ops:
  13.7 5.3 collective-permute-start.1
  19.0 8.9 %rev.15 = f32[128,2048]{1,0:T(8,128)} reverse(f32[128,2048]{1,0:T(8,128)} %param.17), dimensions={0} | reverse | bytes 2097152 | tf_op jit(solution)/shard_map/rev | solution.py:101
  31.3 21.5 %fusion.49 = f32[1,256,2048]{2,0,1:T(1,128)S(1)} fusion(f32[1,383,2048]{2,1,0:T(8,128)S(1)} %convert_multiply_fusion, f32[128,1,2048]{2,0,1:T(8,128)S(1)} %bitcast.140), kind=kOutput, calls=%fused_computation.100 | convolution fusion | flops 805306368 | bytes 6283264 | tf_op jit(solution)/shard_map/conv_general_dilated | solution.py:19
  56.9 7.3 %copy.48 = f32[2,256,2048]{1,0,2:T(2,128)} copy(f32[2,256,2048]{2,1,0:T(8,128)} %pad_maximum_fusion.6) | data formatting | bytes 8388608 | tf_op jit(solution)/shard_map/stack | solution.py:108
  64.1 4.6 all-to-all-start
  68.8 49.0 %all-to-all-done = f32[2,256,2048]{1,0,2:T(2,128)} async-done(((f32[2,256,2048]{1,0,2:T(2,128)}), f32[2,256,2048]{1,0,2:T(2,128)}, u32[]{:S(2)}, u32[]{:S(2)}) %all-to-all-start) | async-done | bytes 4194336 | tf_op jit(solution)/shard_map/all_to_all | solution.py:107
  117.8 9.6 %fusion.58 = (f32[1,8,256,256]{2,0,3,1:T(1,128)}, f32[1,8,256,256]{2,0,3,1:T(1,128)}) fusion(f32[2,8,256,256]{2,0,3,1:T(2,128)} %bitcast.8), kind=kLoop, calls=%fused_computation.113 | loop fusion | bytes 8388608 | tf_op jit(solution)/shard_map/slice | solution.py:115
  127.4 4.5 copy.49
  131.9 6.0 %copy.50 = f32[1,8,256,256]{3,2,1,0:T(8,128)} copy(f32[1,8,256,256]{2,0,3,1:T(1,128)} %get-tuple-element.304) | data formatting | bytes 4194304 | tf_op jit(solution)/shard_map/slice | solution.py:115
  138.0 240.8 %while.19 = (s32[]{:T(128)}, f32[2048,256]{1,0:T(8,128)}, f32[2048,256]{1,0:T(8,128)}, f32[8,256]{1,0:T(8,128)S(1)}, f32[8,256]{1,0:T(8,128)S(1)}, /*index=5*/f3...) while((s32[]{:T(128)}, f32[2048,256]{1,0:T(8,128)}, ...), condition=%wide.region_2.3_spmd.clone.clone, body=%wide.region_0.2_spmd.clone.clone.sunk | while | flops 1617155328 | bytes 74435056 | solution.py:79
  162.0 4.9 fusion.90
  191.0 6.2 %fusion.90 = (f32[2048,256]{1,0:T(8,128)}, f32[2048,256]{1,0:T(8,128)}) fusion(f32[16,128,256]{2,1,0:T(8,128)} %copy.106, f32[2048,256]{1,0:T(8,128)} %get-tuple-element.414, f32[256]{0:T(256)S(1)} %bitcast.142, pred[]{:T(512)S(6)} %compare.24, f32[16,128,256]{2,1,0:T(8,128)} %multiply_add_fusion.22, f32[2048,256]{1,0:T(8,128)} %get-tuple-element.413), kind=kLoop, calls=%fused_computation.3.clone.1 | loop fusion | flops 3145728 | bytes 12583937 | tf_op jit(solution)/shard_map/while/body/eval_jaxpr/add | solution.py:69
  221.3 6.2 %fusion.90 = (f32[2048,256]{1,0:T(8,128)}, f32[2048,256]{1,0:T(8,128)}) fusion(f32[16,128,256]{2,1,0:T(8,128)} %copy.106, f32[2048,256]{1,0:T(8,128)} %get-tuple-element.414, f32[256]{0:T(256)S(1)} %bitcast.142, pred[]{:T(512)S(6)} %compare.24, f32[16,128,256]{2,1,0:T(8,128)} %multiply_add_fusion.22, f32[2048,256]{1,0:T(8,128)} %get-tuple-element.413), kind=kLoop, calls=%fused_computation.3.clone.1 | loop fusion | flops 3145728 | bytes 12583937 | tf_op jit(solution)/shard_map/while/body/eval_jaxpr/add | solution.py:69
  251.5 6.2 %fusion.90 = (f32[2048,256]{1,0:T(8,128)}, f32[2048,256]{1,0:T(8,128)}) fusion(f32[16,128,256]{2,1,0:T(8,128)} %copy.106, f32[2048,256]{1,0:T(8,128)} %get-tuple-element.414, f32[256]{0:T(256)S(1)} %bitcast.142, pred[]{:T(512)S(6)} %compare.24, f32[16,128,256]{2,1,0:T(8,128)} %multiply_add_fusion.22, f32[2048,256]{1,0:T(8,128)} %get-tuple-element.413), kind=kLoop, calls=%fused_computation.3.clone.1 | loop fusion | flops 3145728 | bytes 12583937 | tf_op jit(solution)/shard_map/while/body/eval_jaxpr/add | solution.py:69
  281.8 6.2 %fusion.90 = (f32[2048,256]{1,0:T(8,128)}, f32[2048,256]{1,0:T(8,128)}) fusion(f32[16,128,256]{2,1,0:T(8,128)} %copy.106, f32[2048,256]{1,0:T(8,128)} %get-tuple-element.414, f32[256]{0:T(256)S(1)} %bitcast.142, pred[]{:T(512)S(6)} %compare.24, f32[16,128,256]{2,1,0:T(8,128)} %multiply_add_fusion.22, f32[2048,256]{1,0:T(8,128)} %get-tuple-element.413), kind=kLoop, calls=%fused_computation.3.clone.1 | loop fusion | flops 3145728 | bytes 12583937 | tf_op jit(solution)/shard_map/while/body/eval_jaxpr/add | solution.py:69
  312.0 6.2 %fusion.90 = (f32[2048,256]{1,0:T(8,128)}, f32[2048,256]{1,0:T(8,128)}) fusion(f32[16,128,256]{2,1,0:T(8,128)} %copy.106, f32[2048,256]{1,0:T(8,128)} %get-tuple-element.414, f32[256]{0:T(256)S(1)} %bitcast.142, pred[]{:T(512)S(6)} %compare.24, f32[16,128,256]{2,1,0:T(8,128)} %multiply_add_fusion.22, f32[2048,256]{1,0:T(8,128)} %get-tuple-element.413), kind=kLoop, calls=%fused_computation.3.clone.1 | loop fusion | flops 3145728 | bytes 12583937 | tf_op jit(solution)/shard_map/while/body/eval_jaxpr/add | solution.py:69
  342.3 6.2 %fusion.90 = (f32[2048,256]{1,0:T(8,128)}, f32[2048,256]{1,0:T(8,128)}) fusion(f32[16,128,256]{2,1,0:T(8,128)} %copy.106, f32[2048,256]{1,0:T(8,128)} %get-tuple-element.414, f32[256]{0:T(256)S(1)} %bitcast.142, pred[]{:T(512)S(6)} %compare.24, f32[16,128,256]{2,1,0:T(8,128)} %multiply_add_fusion.22, f32[2048,256]{1,0:T(8,128)} %get-tuple-element.413), kind=kLoop, calls=%fused_computation.3.clone.1 | loop fusion | flops 3145728 | bytes 12583937 | tf_op jit(solution)/shard_map/while/body/eval_jaxpr/add | solution.py:69
  372.6 6.2 %fusion.90 = (f32[2048,256]{1,0:T(8,128)}, f32[2048,256]{1,0:T(8,128)}) fusion(f32[16,128,256]{2,1,0:T(8,128)} %copy.106, f32[2048,256]{1,0:T(8,128)} %get-tuple-element.414, f32[256]{0:T(256)S(1)} %bitcast.142, pred[]{:T(512)S(6)} %compare.24, f32[16,128,256]{2,1,0:T(8,128)} %multiply_add_fusion.22, f32[2048,256]{1,0:T(8,128)} %get-tuple-element.413), kind=kLoop, calls=%fused_computation.3.clone.1 | loop fusion | flops 3145728 | bytes 12583937 | tf_op jit(solution)/shard_map/while/body/eval_jaxpr/add | solution.py:69
  387.8 51.5 %all_to_all.30 = f32[2,2048,256]{2,0,1:T(2,128)S(1)} all-to-all(f32[2,2048,256]{2,0,1:T(2,128)S(1)} %pad_maximum_fusion.7), channel_id=1, replica_groups=mesh['ctx'=8,'tp'=4] {'ctx'}, dimensions={1} | all-to-all | bytes 8388608 | tf_op jit(solution)/shard_map/all_to_all | solution.py:117
  450.9 21.4 %fusion.46 = f32[1,128,2048]{2,0,1:T(1,128)S(1)} fusion(f32[256,1,2048]{2,0,1:T(8,128)S(1)} %bitcast.128, f32[1,383,2048]{2,1,0:T(8,128)S(1)} %copy-done.19), kind=kOutput, calls=%fused_computation.96 | convolution fusion | flops 805306368 | bytes 6283264 | tf_op jit(solution)/shard_map/conv_general_dilated | solution.py:19
  472.7 5.2 rev.16
  477.9 9.9 %all_gather.3 = f32[8,2048]{1,0:T(8,128)S(1)} all-gather(f32[8,256]{1,0:T(8,128)S(1)} %get-tuple-element.201), channel_id=1, replica_groups=mesh['ctx'=8,'tp'=4] {'ctx'}, dimensions={1}, use_global_device_ids=true | all-gather | bytes 73728 | tf_op jit(solution)/shard_map/all_gather | solution.py:122
  488.4 47.4 %all-reduce.20.cloned.1.call-done = f32[128,2048]{1,0:T(8,128)} async-done(((f32[128,2048]{1,0:T(8,128)}), f32[128,2048]{1,0:T(8,128)}) %all-reduce.20.cloned.1.call-update) | async-done | bytes 1048592 | tf_op jit(solution)/shard_map/psum | solution.py:133
  539.7 21.8 %fusion.38 = f32[1,256,2048]{2,0,1:T(1,128)S(1)} fusion(f32[1,383,2048]{2,1,0:T(8,128)S(1)} %maximum_bitcast_fusion, f32[128,1,2048]{2,0,1:T(8,128)S(1)} %bitcast.139), kind=kOutput, calls=%fused_computation.81 | convolution fusion | flops 805306368 | bytes 6283264 | tf_op jit(solution)/shard_map/conv_general_dilated | solution.py:19
  (758 shorter events, 220.5 us)
Async XLA Ops:
  7.2 61.6 %copy-start = (f32[8,2048]{1,0:T(8,128)S(1)}, f32[8,2048]{1,0:T(8,128)}, u32[]{:S(2)}) copy-start(f32[8,2048]{1,0:T(8,128)} %param.19) | copy-start | bytes 196612
  7.2 20.7 %copy-start.9 = (bf16[256,2048]{1,0:T(8,128)(2,1)S(1)}, bf16[256,2048]{1,0:T(8,128)(2,1)}, u32[]{:S(2)}) copy-start(bf16[256,2048]{1,0:T(8,128)(2,1)} %param.12) | copy-start | bytes 3145732
  7.2 20.7 %copy-start.11 = (bf16[256,2048]{1,0:T(8,128)(2,1)S(1)}, bf16[256,2048]{1,0:T(8,128)(2,1)}, u32[]{:S(2)}) copy-start(bf16[256,2048]{1,0:T(8,128)(2,1)} %param.13) | copy-start | bytes 3145732
  9.3 18.5 %collective-permute-start = (bf16[127,2048]{1,0:T(8,128)(2,1)}, bf16[127,2048]{1,0:T(8,128)(2,1)S(1)}, u32[]{:S(2)}, u32[]{:S(2)}) collective-permute-start(bf16[127,2048]{1,0:T(8,128)(2,1)} %slice.393), channel_id=1, source_target_pairs={{0,4},{4,8},{8,12},{12,16},{16,20},{20,24},{24,28},{1,5},{5,9},{9,... | collective-permute-start | bytes 1560584 | tf_op jit(solution)/shard_map/ppermute | solution.py:14
  13.7 14.1 %collective-permute-start.1 = (bf16[127,2048]{1,0:T(8,128)(2,1)}, bf16[127,2048]{1,0:T(8,128)(2,1)}, u32[]{:S(2)}, u32[]{:S(2)}) collective-permute-start(bf16[127,2048]{1,0:T(8,128)(2,1)} %slice.394), channel_id=1, source_target_pairs={{0,4},{4,8},{8,12},{12,16},{16,20},{20,24},{24,28},{1,5},{5,9},{9,... | collective-permute-start | bytes 1560584 | tf_op jit(solution)/shard_map/ppermute | solution.py:14
  31.3 21.6 %copy-start.13 = (bf16[256,2048]{1,0:T(8,128)(2,1)S(1)}, bf16[256,2048]{1,0:T(8,128)(2,1)}, u32[]{:S(2)}) copy-start(bf16[256,2048]{1,0:T(8,128)(2,1)} %param.15) | copy-start | bytes 3145732
  31.3 21.6 %copy-start.14 = (bf16[256,2048]{1,0:T(8,128)(2,1)S(1)}, bf16[256,2048]{1,0:T(8,128)(2,1)}, u32[]{:S(2)}) copy-start(bf16[256,2048]{1,0:T(8,128)(2,1)} %param.11) | copy-start | bytes 3145732
  31.3 21.6 %copy-start.16 = (bf16[256,2048]{1,0:T(8,128)(2,1)S(1)}, bf16[256,2048]{1,0:T(8,128)(2,1)}, u32[]{:S(2)}) copy-start(bf16[256,2048]{1,0:T(8,128)(2,1)} %param.16) | copy-start | bytes 3145732
  31.3 21.6 %copy-start.20 = (bf16[256,2048]{1,0:T(8,128)(2,1)S(1)}, bf16[256,2048]{1,0:T(8,128)(2,1)}, u32[]{:S(2)}) copy-start(bf16[256,2048]{1,0:T(8,128)(2,1)} %param.14) | copy-start | bytes 3145732
  64.1 53.7 %all-to-all-start = ((f32[2,256,2048]{1,0,2:T(2,128)}), f32[2,256,2048]{1,0,2:T(2,128)}, u32[]{:S(2)}, u32[]{:S(2)}) async-start(f32[2,256,2048]{1,0,2:T(2,128)} %copy.48), calls=%async_computation | async-start | bytes 8388608 | tf_op jit(solution)/shard_map/all_to_all | solution.py:107
  68.7 467.2 %all-reduce.20.cloned.1.call-start = ((), (), s32[]{:S(2)}) async-start(), calls=%async_computation.2 | async-start | bytes 2097152 | tf_op jit(solution)/shard_map/psum | solution.py:133
  131.9 6.1 %copy-start.23 = (f32[8]{0:T(128)S(1)}, f32[8]{0:T(128)}, u32[]{:S(2)}) copy-start(f32[8]{0:T(128)} %param.18) | copy-start | bytes 100
  191.0 6.2 %copy-start.3 = (f32[2048,256]{1,0:T(8,128)S(1)}, f32[2048,256]{1,0:T(8,128)}, u32[]{:S(2)}) copy-start(f32[2048,256]{1,0:T(8,128)} %copy-done.2) | copy-start | bytes 6291460 | tf_op jit(solution)/shard_map/while
  221.3 6.2 %copy-start.3 = (f32[2048,256]{1,0:T(8,128)S(1)}, f32[2048,256]{1,0:T(8,128)}, u32[]{:S(2)}) copy-start(f32[2048,256]{1,0:T(8,128)} %copy-done.2) | copy-start | bytes 6291460 | tf_op jit(solution)/shard_map/while
  251.5 6.2 %copy-start.3 = (f32[2048,256]{1,0:T(8,128)S(1)}, f32[2048,256]{1,0:T(8,128)}, u32[]{:S(2)}) copy-start(f32[2048,256]{1,0:T(8,128)} %copy-done.2) | copy-start | bytes 6291460 | tf_op jit(solution)/shard_map/while
  281.8 6.2 %copy-start.3 = (f32[2048,256]{1,0:T(8,128)S(1)}, f32[2048,256]{1,0:T(8,128)}, u32[]{:S(2)}) copy-start(f32[2048,256]{1,0:T(8,128)} %copy-done.2) | copy-start | bytes 6291460 | tf_op jit(solution)/shard_map/while
  312.0 6.2 %copy-start.3 = (f32[2048,256]{1,0:T(8,128)S(1)}, f32[2048,256]{1,0:T(8,128)}, u32[]{:S(2)}) copy-start(f32[2048,256]{1,0:T(8,128)} %copy-done.2) | copy-start | bytes 6291460 | tf_op jit(solution)/shard_map/while
  342.3 6.2 %copy-start.3 = (f32[2048,256]{1,0:T(8,128)S(1)}, f32[2048,256]{1,0:T(8,128)}, u32[]{:S(2)}) copy-start(f32[2048,256]{1,0:T(8,128)} %copy-done.2) | copy-start | bytes 6291460 | tf_op jit(solution)/shard_map/while
  372.6 6.2 %copy-start.3 = (f32[2048,256]{1,0:T(8,128)S(1)}, f32[2048,256]{1,0:T(8,128)}, u32[]{:S(2)}) copy-start(f32[2048,256]{1,0:T(8,128)} %copy-done.2) | copy-start | bytes 6291460 | tf_op jit(solution)/shard_map/while
  445.1 5.8 %copy-start.19 = (f32[1,383,2048]{2,1,0:T(8,128)S(1)}, f32[1,383,2048]{2,1,0:T(8,128)}, u32[]{:S(2)}) copy-start(f32[1,383,2048]{2,1,0:T(8,128)} %copy-done.18) | copy-start | bytes 9412612
  449.6 88.5 %collective-permute-start.2 = (f32[127,2048]{1,0:T(8,128)}, f32[127,2048]{1,0:T(8,128)}, u32[]{:S(2)}, u32[]{:S(2)}) collective-permute-start(f32[127,2048]{1,0:T(8,128)} %slice.517), channel_id=1, source_target_pairs={{4,0},{8,4},{12,8},{16,12},{20,16},{24,20},{28,24},{5,1},{9,5},{13... | collective-permute-start | bytes 3121160 | tf_op jit(solution)/shard_map/ppermute | solution.py:14
  539.7 21.8 %copy-start.10 = (bf16[256,2048]{1,0:T(8,128)(2,1)S(1)}, bf16[256,2048]{1,0:T(8,128)(2,1)}, u32[]{:S(2)}) copy-start(bf16[256,2048]{1,0:T(8,128)(2,1)} %param.12) | copy-start | bytes 3145732
  539.7 21.8 %copy-start.12 = (bf16[256,2048]{1,0:T(8,128)(2,1)S(1)}, bf16[256,2048]{1,0:T(8,128)(2,1)}, u32[]{:S(2)}) copy-start(bf16[256,2048]{1,0:T(8,128)(2,1)} %param.13) | copy-start | bytes 3145732
  539.7 24.3 %copy-start.1 = (f32[8,2048]{1,0:T(8,128)S(1)}, f32[8,2048]{1,0:T(8,128)}, u32[]{:S(2)}) copy-start(f32[8,2048]{1,0:T(8,128)} %param.19) | copy-start | bytes 196612
  (33 other events, 76.4 us)
Sparse Core Ops, SparseCore 0:
  478.0 57.7 all-reduce.19
where the time goes:
time: 574 us; the launch traced here: 571 us
  local copies, waits for them, and re-layouts  134 us (23%)
  other arithmetic  128 us (22%)
  matrix products  108 us (19%)
  waiting for transfers between devices  96.4 us (17%)
  blocking collectives  61.4 us (11%)
  between operations  14.4 us (3%)
  loops' own time  13.9 us (2%)
  starting transfers between devices  13.6 us (2%)
    conv_general_dilated x3, matrix products, depthwise(): lax.conv_general_dilated(signal[None], kernel[:, None, :], (1,), 'VALID',...  64.7 us
    all_to_all x1, blocking collectives, per_device(): lax.all_to_all(jnp.stack([conv_seq, back_seq]), 'ctx', split_axis=1, conc...  51.5 us
    all_to_all x1, waiting for transfers between devices, per_device(): lax.all_to_all(jnp.stack([li_input, li_cotan]), 'ctx', split_axis=2, conc...  49 us
    add x8, other arithmetic, one_mode(): back_sum = back_sum + residue_row[None, :] * reverse_states  48.2 us
    psum x1, waiting for transfers between devices, per_device(): tap_sum = lax.psum(tap_part, 'ctx')  47.4 us
    reduce_sum x8, other arithmetic, one_mode(): jnp.sum(inputs * reverse_states, 0)  32.1 us
    dot_general x8, matrix products, one_mode(): backward = jnp.einsum('jt,bjc->btc', toeplitz, co_blocks, precision=highest)  27.8 us
    add x8, other arithmetic, one_mode(): forward + lead_pows[None, :, None] * forward_in[:, None, :]  26.2 us
  transfers between devices with their start and end apart: 5, of which 2 were waited for; matrix products, arithmetic and copies ran while one was open for 7% of the time, Pallas kernels for 0%

commit v1 on v0

--- a/solution.py
+++ b/solution.py
@@ -104,9 +104,16 @@
     cotan = cotangent.astype(jnp.float32)
     li_input = key_second * mr_out
     li_cotan = cotan * query_li.astype(jnp.float32)
-    regrouped = lax.all_to_all(
-        jnp.stack([li_input, li_cotan]), "ctx", split_axis=2, concat_axis=1, tiled=True
-    )
+    x = jnp.stack([li_input, li_cotan])
+    ways, here = (lax.axis_size("ctx"), lax.axis_index("ctx"))
+    width = x.shape[2] // ways
+    turned = jnp.roll(x, -here * width, axis=2)
+    got = [lax.slice_in_dim(turned, 0, width, axis=2)]
+    for far in range(1, ways):
+        sent = lax.slice_in_dim(turned, far * width, (far + 1) * width, axis=2)
+        got.append(lax.ppermute(sent, "ctx", [(d, (d + far) % ways) for d in range(ways)]))
+    line = jnp.concatenate(got[::-1], axis=1)
+    regrouped = jnp.roll(line, (here + 1) * got[0].shape[1], axis=1)
     piece_cols = channels // devices_ctx
     local_residues = lax.dynamic_slice_in_dim(
         residues, lax.axis_index("ctx") * piece_cols, piece_cols, 1

time: 574 us -> 548 us (0.955)
  local copies, waits for them, and re-layouts: 134 us -> 116 us
  waiting for transfers between devices: 96.4 us -> 90.3 us
    all_to_all x1 -> x0, waiting for transfers between devices: 49 us -> none  [per_device(): lax.all_to_all(jnp.stack([li_input, li_cotan]), 'ctx', split_axis=2, conc...]
    ppermute x0 -> x7, waiting for transfers between devices: none -> 42.8 us  [per_device(): lax.ppermute(sent, 'ctx', [(d, (d + far) % ways) for d in range(ways)])]
    slice x2 -> x1, local copies, waits for them, and re-layouts: 15.6 us -> 1.69 us  [per_device(): regrouped[1]]
    ppermute x0 -> x7, starting transfers between devices: none -> 8.08 us  [per_device(): lax.ppermute(sent, 'ctx', [(d, (d + far) % ways) for d in range(ways)])]
    another operation x1 -> x0, local copies, waits for them, and re-layouts: 7.26 us -> none  [per_device(): jnp.stack([li_input, li_cotan])]
  transfers between devices with their start and end apart: 5 -> 11, of which waited for: 2 -> 5; matrix products, arithmetic and copies ran while one was open for 7% -> 8% of each run, Pallas kernels for 0% -> 0%
where the time goes in v1:
time: 548 us; the launch traced here: 546 us
  other arithmetic  125 us (23%)
  local copies, waits for them, and re-layouts  116 us (21%)
  matrix products  108 us (20%)
  waiting for transfers between devices  90.3 us (16%)
  blocking collectives  61.4 us (11%)
  starting transfers between devices  16.3 us (3%)
  between operations  14.6 us (3%)
  loops' own time  14 us (3%)
    conv_general_dilated x3, matrix products, depthwise(): lax.conv_general_dilated(signal[None], kernel[:, None, :], (1,), 'VALID',...  64.7 us
    all_to_all x1, blocking collectives, per_device(): lax.all_to_all(jnp.stack([conv_seq, back_seq]), 'ctx', split_axis=1, conc...  51.5 us
    add x8, other arithmetic, one_mode(): back_sum = back_sum + residue_row[None, :] * reverse_states  48.5 us
    psum x1, waiting for transfers between devices, per_device(): tap_sum = lax.psum(tap_part, 'ctx')  47.4 us
    ppermute x7, waiting for transfers between devices, per_device(): lax.ppermute(sent, 'ctx', [(d, (d + far) % ways) for d in range(ways)])  42.8 us
    reduce_sum x8, other arithmetic, one_mode(): jnp.sum(inputs * reverse_states, 0)  32 us
    dot_general x8, matrix products, one_mode(): backward = jnp.einsum('jt,bjc->btc', toeplitz, co_blocks, precision=highest)  27.8 us
    add x8, other arithmetic, one_mode(): forward + lead_pows[None, :, None] * forward_in[:, None, :]  25.5 us
  transfers between devices with their start and end apart: 11, of which 5 were waited for; matrix products, arithmetic and copies ran while one was open for 8% of the time, Pallas kernels for 0%

profile of v1, /device:TPU:0, one launch (start us, length us, event | category | flops | bytes accessed | tf_op | source)
XLA Modules:
  0.0 545.7 jit_solution(6562317067519555209)
XLA Ops:
  13.8 4.5 collective-permute-start.1
  18.3 8.9 %rev.15 = f32[128,2048]{1,0:T(8,128)} reverse(f32[128,2048]{1,0:T(8,128)} %param.17), dimensions={0} | reverse | bytes 2097152 | tf_op jit(solution)/shard_map/rev | solution.py:101
  29.5 21.5 %fusion.52 = f32[1,256,2048]{2,0,1:T(1,128)S(1)} fusion(f32[1,383,2048]{2,1,0:T(8,128)S(1)} %convert_multiply_fusion, f32[128,1,2048]{2,0,1:T(8,128)S(1)} %bitcast.137), kind=kOutput, calls=%fused_computation.106 | convolution fusion | flops 805306368 | bytes 6283264 | tf_op jit(solution)/shard_map/conv_general_dilated | solution.py:19
  61.1 6.2 %collective-permute-done.2 = f32[2,256,256]{2,1,0:T(8,128)S(1)} collective-permute-done((f32[2,256,256]{2,1,0:T(8,128)}, f32[2,256,256]{2,1,0:T(8,128)S(1)}, u32[]{:S(2)}, u32[]{:S(2)}) %collective-permute-start.2) | collective-permute-done | bytes 524320 | tf_op jit(solution)/shard_map/ppermute | solution.py:114
  70.9 11.5 %collective-permute-done.3 = f32[2,256,256]{2,1,0:T(8,128)S(1)} collective-permute-done((f32[2,256,256]{2,1,0:T(8,128)}, f32[2,256,256]{2,1,0:T(8,128)S(1)}, u32[]{:S(2)}, u32[]{:S(2)}) %collective-permute-start.3) | collective-permute-done | bytes 524320 | tf_op jit(solution)/shard_map/ppermute | solution.py:114
  82.5 24.2 %collective-permute-done.5 = f32[2,256,256]{2,1,0:T(8,128)S(1)} collective-permute-done((f32[2,256,256]{2,1,0:T(8,128)}, f32[2,256,256]{2,1,0:T(8,128)S(1)}, u32[]{:S(2)}, u32[]{:S(2)}) %collective-permute-start.5) | collective-permute-done | bytes 524320 | tf_op jit(solution)/shard_map/ppermute | solution.py:114
  114.1 239.6 %while.19 = (s32[]{:T(128)}, f32[2048,256]{1,0:T(8,128)}, f32[2048,256]{1,0:T(8,128)}, f32[8,256]{1,0:T(8,128)S(1)}, f32[8,256]{1,0:T(8,128)S(1)}, /*index=5*/f3...) while((s32[]{:T(128)}, f32[2048,256]{1,0:T(8,128)}, ...), condition=%wide.region_2.3_spmd.clone.clone, body=%wide.region_0.2_spmd.clone.clone.sunk | while | flops 1617155328 | bytes 74435056 | solution.py:79
  131.3 4.0 fusion.92
  137.9 5.0 fusion.93
  160.2 4.0 fusion.92
  166.8 6.2 %fusion.93 = (f32[2048,256]{1,0:T(8,128)}, f32[2048,256]{1,0:T(8,128)}) fusion(f32[16,128,256]{2,1,0:T(8,128)} %copy.96, f32[2048,256]{1,0:T(8,128)} %get-tuple-element.421, f32[256]{0:T(256)S(1)} %bitcast.140, pred[]{:T(512)S(6)} %compare.26, f32[16,128,256]{2,1,0:T(8,128)} %multiply_add_fusion.22, f32[2048,256]{1,0:T(8,128)} %get-tuple-element.420), kind=kLoop, calls=%fused_computation.3.clone.1 | loop fusion | flops 3145728 | bytes 12583937 | tf_op jit(solution)/shard_map/while/body/eval_jaxpr/add | solution.py:69
  196.9 6.2 %fusion.93 = (f32[2048,256]{1,0:T(8,128)}, f32[2048,256]{1,0:T(8,128)}) fusion(f32[16,128,256]{2,1,0:T(8,128)} %copy.96, f32[2048,256]{1,0:T(8,128)} %get-tuple-element.421, f32[256]{0:T(256)S(1)} %bitcast.140, pred[]{:T(512)S(6)} %compare.26, f32[16,128,256]{2,1,0:T(8,128)} %multiply_add_fusion.22, f32[2048,256]{1,0:T(8,128)} %get-tuple-element.420), kind=kLoop, calls=%fused_computation.3.clone.1 | loop fusion | flops 3145728 | bytes 12583937 | tf_op jit(solution)/shard_map/while/body/eval_jaxpr/add | solution.py:69
  227.0 6.2 %fusion.93 = (f32[2048,256]{1,0:T(8,128)}, f32[2048,256]{1,0:T(8,128)}) fusion(f32[16,128,256]{2,1,0:T(8,128)} %copy.96, f32[2048,256]{1,0:T(8,128)} %get-tuple-element.421, f32[256]{0:T(256)S(1)} %bitcast.140, pred[]{:T(512)S(6)} %compare.26, f32[16,128,256]{2,1,0:T(8,128)} %multiply_add_fusion.22, f32[2048,256]{1,0:T(8,128)} %get-tuple-element.420), kind=kLoop, calls=%fused_computation.3.clone.1 | loop fusion | flops 3145728 | bytes 12583937 | tf_op jit(solution)/shard_map/while/body/eval_jaxpr/add | solution.py:69
  257.1 6.2 %fusion.93 = (f32[2048,256]{1,0:T(8,128)}, f32[2048,256]{1,0:T(8,128)}) fusion(f32[16,128,256]{2,1,0:T(8,128)} %copy.96, f32[2048,256]{1,0:T(8,128)} %get-tuple-element.421, f32[256]{0:T(256)S(1)} %bitcast.140, pred[]{:T(512)S(6)} %compare.26, f32[16,128,256]{2,1,0:T(8,128)} %multiply_add_fusion.22, f32[2048,256]{1,0:T(8,128)} %get-tuple-element.420), kind=kLoop, calls=%fused_computation.3.clone.1 | loop fusion | flops 3145728 | bytes 12583937 | tf_op jit(solution)/shard_map/while/body/eval_jaxpr/add | solution.py:69
  287.2 6.2 %fusion.93 = (f32[2048,256]{1,0:T(8,128)}, f32[2048,256]{1,0:T(8,128)}) fusion(f32[16,128,256]{2,1,0:T(8,128)} %copy.96, f32[2048,256]{1,0:T(8,128)} %get-tuple-element.421, f32[256]{0:T(256)S(1)} %bitcast.140, pred[]{:T(512)S(6)} %compare.26, f32[16,128,256]{2,1,0:T(8,128)} %multiply_add_fusion.22, f32[2048,256]{1,0:T(8,128)} %get-tuple-element.420), kind=kLoop, calls=%fused_computation.3.clone.1 | loop fusion | flops 3145728 | bytes 12583937 | tf_op jit(solution)/shard_map/while/body/eval_jaxpr/add | solution.py:69
  317.4 6.2 %fusion.93 = (f32[2048,256]{1,0:T(8,128)}, f32[2048,256]{1,0:T(8,128)}) fusion(f32[16,128,256]{2,1,0:T(8,128)} %copy.96, f32[2048,256]{1,0:T(8,128)} %get-tuple-element.421, f32[256]{0:T(256)S(1)} %bitcast.140, pred[]{:T(512)S(6)} %compare.26, f32[16,128,256]{2,1,0:T(8,128)} %multiply_add_fusion.22, f32[2048,256]{1,0:T(8,128)} %get-tuple-element.420), kind=kLoop, calls=%fused_computation.3.clone.1 | loop fusion | flops 3145728 | bytes 12583937 | tf_op jit(solution)/shard_map/while/body/eval_jaxpr/add | solution.py:69
  347.5 6.2 %fusion.93 = (f32[2048,256]{1,0:T(8,128)}, f32[2048,256]{1,0:T(8,128)}) fusion(f32[16,128,256]{2,1,0:T(8,128)} %copy.96, f32[2048,256]{1,0:T(8,128)} %get-tuple-element.421, f32[256]{0:T(256)S(1)} %bitcast.140, pred[]{:T(512)S(6)} %compare.26, f32[16,128,256]{2,1,0:T(8,128)} %multiply_add_fusion.22, f32[2048,256]{1,0:T(8,128)} %get-tuple-element.420), kind=kLoop, calls=%fused_computation.3.clone.1 | loop fusion | flops 3145728 | bytes 12583937 | tf_op jit(solution)/shard_map/while/body/eval_jaxpr/add | solution.py:69
  358.7 4.1 pad_maximum_fusion.6
  362.8 51.5 %all_to_all.15 = f32[2,2048,256]{2,0,1:T(2,128)S(1)} all-to-all(f32[2,2048,256]{2,0,1:T(2,128)S(1)} %pad_maximum_fusion.6), channel_id=1, replica_groups=mesh['ctx'=8,'tp'=4] {'ctx'}, dimensions={1} | all-to-all | bytes 8388608 | tf_op jit(solution)/shard_map/all_to_all | solution.py:124
  425.8 21.4 %fusion.49 = f32[1,128,2048]{2,0,1:T(1,128)S(1)} fusion(f32[256,1,2048]{2,0,1:T(8,128)S(1)} %bitcast.125, f32[1,383,2048]{2,1,0:T(8,128)S(1)} %copy-done.20), kind=kOutput, calls=%fused_computation.102 | convolution fusion | flops 805306368 | bytes 6283264 | tf_op jit(solution)/shard_map/conv_general_dilated | solution.py:19
  447.5 5.2 rev.16
  452.7 9.9 %all_gather.3 = f32[8,2048]{1,0:T(8,128)S(1)} all-gather(f32[8,256]{1,0:T(8,128)S(1)} %get-tuple-element.201), channel_id=1, replica_groups=mesh['ctx'=8,'tp'=4] {'ctx'}, dimensions={1}, use_global_device_ids=true | all-gather | bytes 73728 | tf_op jit(solution)/shard_map/all_gather | solution.py:129
  463.2 47.4 %all-reduce.20.cloned.1.call-done = f32[128,2048]{1,0:T(8,128)} async-done(((f32[128,2048]{1,0:T(8,128)}), f32[128,2048]{1,0:T(8,128)}) %all-reduce.20.cloned.1.call-update) | async-done | bytes 1048592 | tf_op jit(solution)/shard_map/psum | solution.py:140
  514.6 21.8 %fusion.41 = f32[1,256,2048]{2,0,1:T(1,128)S(1)} fusion(f32[1,383,2048]{2,1,0:T(8,128)S(1)} %maximum_bitcast_fusion, f32[128,1,2048]{2,0,1:T(8,128)S(1)} %bitcast.136), kind=kOutput, calls=%fused_computation.87 | convolution fusion | flops 805306368 | bytes 6283264 | tf_op jit(solution)/shard_map/conv_general_dilated | solution.py:19
  (786 shorter events, 222.6 us)
Async XLA Ops:
  7.2 54.0 %copy-start = (f32[8,2048]{1,0:T(8,128)S(1)}, f32[8,2048]{1,0:T(8,128)}, u32[]{:S(2)}) copy-start(f32[8,2048]{1,0:T(8,128)} %param.19) | copy-start | bytes 196612
  7.2 20.0 %copy-start.10 = (bf16[256,2048]{1,0:T(8,128)(2,1)S(1)}, bf16[256,2048]{1,0:T(8,128)(2,1)}, u32[]{:S(2)}) copy-start(bf16[256,2048]{1,0:T(8,128)(2,1)} %param.12) | copy-start | bytes 3145732
  7.2 20.0 %copy-start.12 = (bf16[256,2048]{1,0:T(8,128)(2,1)S(1)}, bf16[256,2048]{1,0:T(8,128)(2,1)}, u32[]{:S(2)}) copy-start(bf16[256,2048]{1,0:T(8,128)(2,1)} %param.13) | copy-start | bytes 3145732
  7.2 503.5 %all-reduce.20.cloned.1.call-start = ((), (), s32[]{:S(2)}) async-start(), calls=%async_computation.1 | async-start | bytes 2097152 | tf_op jit(solution)/shard_map/psum | solution.py:140
  9.4 17.8 %collective-permute-start = (bf16[127,2048]{1,0:T(8,128)(2,1)}, bf16[127,2048]{1,0:T(8,128)(2,1)S(1)}, u32[]{:S(2)}, u32[]{:S(2)}) collective-permute-start(bf16[127,2048]{1,0:T(8,128)(2,1)} %slice.415), channel_id=1, source_target_pairs={{0,4},{4,8},{8,12},{12,16},{16,20},{20,24},{24,28},{1,5},{5,9},{9,... | collective-permute-start | bytes 1560584 | tf_op jit(solution)/shard_map/ppermute | solution.py:14
  13.8 13.4 %collective-permute-start.1 = (bf16[127,2048]{1,0:T(8,128)(2,1)}, bf16[127,2048]{1,0:T(8,128)(2,1)S(1)}, u32[]{:S(2)}, u32[]{:S(2)}) collective-permute-start(bf16[127,2048]{1,0:T(8,128)(2,1)} %slice.416), channel_id=1, source_target_pairs={{0,4},{4,8},{8,12},{12,16},{16,20},{20,24},{24,28},{1,5},{5,9},{9,... | collective-permute-start | bytes 1560584 | tf_op jit(solution)/shard_map/ppermute | solution.py:14
  29.5 21.6 %copy-start.14 = (bf16[256,2048]{1,0:T(8,128)(2,1)S(1)}, bf16[256,2048]{1,0:T(8,128)(2,1)}, u32[]{:S(2)}) copy-start(bf16[256,2048]{1,0:T(8,128)(2,1)} %param.15) | copy-start | bytes 3145732
  29.5 21.6 %copy-start.15 = (bf16[256,2048]{1,0:T(8,128)(2,1)S(1)}, bf16[256,2048]{1,0:T(8,128)(2,1)}, u32[]{:S(2)}) copy-start(bf16[256,2048]{1,0:T(8,128)(2,1)} %param.11) | copy-start | bytes 3145732
  29.5 21.6 %copy-start.17 = (bf16[256,2048]{1,0:T(8,128)(2,1)S(1)}, bf16[256,2048]{1,0:T(8,128)(2,1)}, u32[]{:S(2)}) copy-start(bf16[256,2048]{1,0:T(8,128)(2,1)} %param.16) | copy-start | bytes 3145732
  29.5 21.6 %copy-start.21 = (bf16[256,2048]{1,0:T(8,128)(2,1)S(1)}, bf16[256,2048]{1,0:T(8,128)(2,1)}, u32[]{:S(2)}) copy-start(bf16[256,2048]{1,0:T(8,128)(2,1)} %param.14) | copy-start | bytes 3145732
  56.6 10.7 %collective-permute-start.2 = (f32[2,256,256]{2,1,0:T(8,128)}, f32[2,256,256]{2,1,0:T(8,128)S(1)}, u32[]{:S(2)}, u32[]{:S(2)}) collective-permute-start(f32[2,256,256]{2,1,0:T(8,128)} %get-tuple-element.312), channel_id=1, source_target_pairs={{0,28},{4,0},{8,4},{12,8},{16,12},{20,16},{24,20},{28,24},{1,29},{... | collective-permute-start | bytes 1572872 | tf_op jit(solution)/shard_map/ppermute | solution.py:114
  56.6 25.8 %collective-permute-start.3 = (f32[2,256,256]{2,1,0:T(8,128)}, f32[2,256,256]{2,1,0:T(8,128)S(1)}, u32[]{:S(2)}, u32[]{:S(2)}) collective-permute-start(f32[2,256,256]{2,1,0:T(8,128)} %get-tuple-element.311), channel_id=1, source_target_pairs={{0,24},{4,28},{8,0},{12,4},{16,8},{20,12},{24,16},{28,20},{1,25},{... | collective-permute-start | bytes 1572872 | tf_op jit(solution)/shard_map/ppermute | solution.py:114
  59.2 23.3 %collective-permute-start.4 = (f32[2,256,256]{2,1,0:T(8,128)}, f32[2,256,256]{2,1,0:T(8,128)S(1)}, u32[]{:S(2)}, u32[]{:S(2)}) collective-permute-start(f32[2,256,256]{2,1,0:T(8,128)} %get-tuple-element.310), channel_id=1, source_target_pairs={{0,20},{4,24},{8,28},{12,0},{16,4},{20,8},{24,12},{28,16},{1,21},{... | collective-permute-start | bytes 1572872 | tf_op jit(solution)/shard_map/ppermute | solution.py:114
  59.4 47.3 %collective-permute-start.5 = (f32[2,256,256]{2,1,0:T(8,128)}, f32[2,256,256]{2,1,0:T(8,128)S(1)}, u32[]{:S(2)}, u32[]{:S(2)}) collective-permute-start(f32[2,256,256]{2,1,0:T(8,128)} %get-tuple-element.309), channel_id=1, source_target_pairs={{0,16},{4,20},{8,24},{12,28},{16,0},{20,4},{24,8},{28,12},{1,17},{... | collective-permute-start | bytes 1572872 | tf_op jit(solution)/shard_map/ppermute | solution.py:114
  60.9 46.8 %collective-permute-start.6 = (f32[2,256,256]{2,1,0:T(8,128)}, f32[2,256,256]{2,1,0:T(8,128)}, u32[]{:S(2)}, u32[]{:S(2)}) collective-permute-start(f32[2,256,256]{2,1,0:T(8,128)} %get-tuple-element.308), channel_id=1, source_target_pairs={{0,12},{4,16},{8,20},{12,24},{16,28},{20,0},{24,4},{28,8},{1,13},{... | collective-permute-start | bytes 1572872 | tf_op jit(solution)/shard_map/ppermute | solution.py:114
  67.3 41.5 %collective-permute-start.7 = (f32[2,256,256]{2,1,0:T(8,128)}, f32[2,256,256]{2,1,0:T(8,128)S(1)}, u32[]{:S(2)}, u32[]{:S(2)}) collective-permute-start(f32[2,256,256]{2,1,0:T(8,128)} %get-tuple-element.307), channel_id=1, source_target_pairs={{0,8},{4,12},{8,16},{12,20},{16,24},{20,28},{24,0},{28,4},{1,9},{5... | collective-permute-start | bytes 1572872 | tf_op jit(solution)/shard_map/ppermute | solution.py:114
  82.4 26.4 %collective-permute-start.8 = (f32[2,256,256]{2,1,0:T(8,128)}, f32[2,256,256]{2,1,0:T(8,128)S(1)}, u32[]{:S(2)}, u32[]{:S(2)}) collective-permute-start(f32[2,256,256]{2,1,0:T(8,128)} %get-tuple-element.306), channel_id=1, source_target_pairs={{0,4},{4,8},{8,12},{12,16},{16,20},{20,24},{24,28},{28,0},{1,5},{5... | collective-permute-start | bytes 1572872 | tf_op jit(solution)/shard_map/ppermute | solution.py:114
  166.8 6.3 %copy-start.3 = (f32[2048,256]{1,0:T(8,128)S(1)}, f32[2048,256]{1,0:T(8,128)}, u32[]{:S(2)}) copy-start(f32[2048,256]{1,0:T(8,128)} %copy-done.2) | copy-start | bytes 6291460 | tf_op jit(solution)/shard_map/while
  196.9 6.3 %copy-start.3 = (f32[2048,256]{1,0:T(8,128)S(1)}, f32[2048,256]{1,0:T(8,128)}, u32[]{:S(2)}) copy-start(f32[2048,256]{1,0:T(8,128)} %copy-done.2) | copy-start | bytes 6291460 | tf_op jit(solution)/shard_map/while
  227.0 6.3 %copy-start.3 = (f32[2048,256]{1,0:T(8,128)S(1)}, f32[2048,256]{1,0:T(8,128)}, u32[]{:S(2)}) copy-start(f32[2048,256]{1,0:T(8,128)} %copy-done.2) | copy-start | bytes 6291460 | tf_op jit(solution)/shard_map/while
  424.5 88.5 %collective-permute-start.9 = (f32[127,2048]{1,0:T(8,128)}, f32[127,2048]{1,0:T(8,128)}, u32[]{:S(2)}, u32[]{:S(2)}) collective-permute-start(f32[127,2048]{1,0:T(8,128)} %slice.553), channel_id=1, source_target_pairs={{4,0},{8,4},{12,8},{16,12},{20,16},{24,20},{28,24},{5,1},{9,5},{13... | collective-permute-start | bytes 3121160 | tf_op jit(solution)/shard_map/ppermute | solution.py:14
  514.5 21.8 %copy-start.11 = (bf16[256,2048]{1,0:T(8,128)(2,1)S(1)}, bf16[256,2048]{1,0:T(8,128)(2,1)}, u32[]{:S(2)}) copy-start(bf16[256,2048]{1,0:T(8,128)(2,1)} %param.12) | copy-start | bytes 3145732
  514.6 21.8 %copy-start.13 = (bf16[256,2048]{1,0:T(8,128)(2,1)S(1)}, bf16[256,2048]{1,0:T(8,128)(2,1)}, u32[]{:S(2)}) copy-start(bf16[256,2048]{1,0:T(8,128)(2,1)} %param.13) | copy-start | bytes 3145732
  514.6 24.3 %copy-start.1 = (f32[8,2048]{1,0:T(8,128)S(1)}, f32[8,2048]{1,0:T(8,128)}, u32[]{:S(2)}) copy-start(f32[8,2048]{1,0:T(8,128)} %param.19) | copy-start | bytes 196612
  (40 other events, 110.5 us)
Sparse Core Ops, SparseCore 0:
  452.9 57.7 all-reduce.19
